TPU v7x, 256 devices: a whole 4x4x8 slice. The times are simulated.
256 devices in a mesh: row: 32 (over y, z), col: 8 (over x, core).
Axes of the slice: x: 4, y: 4, z: 8, core: 2. Of those that a mesh axis runs over, the one named last changes fastest.
Arguments:
- lower: float32 [6, 2048, 2048], P(None, 'row', 'col'), may hold values from -0.046875 to 0.046875
- dinv: float32 [4, 2048, 2048], P(None, 'row', 'col'), as said below
- kcols: float32 [4, 2048, 2048], P(None, 'row', 'col'), may hold values from -6 to 6
- prior: float32 [2048], P('col'), may hold values from 3 to 5
Outputs:
- solved_columns: float32 [4, 2048, 2048], P(None, 'row', 'col')
- variance: float32 [2048], P('col')
Inputs may be any that keep to these rules, and one draw needn't show every extreme that they name: Each block of dinv is lower triangular with a positive diagonal.
All inputs are finite; a program needn't handle non-finite values.
Results may differ from a plain program's by a relative error of at most 0.0001.
Values sent between devices are 32-bit elements; how exact they have to be, the bound alone decides.
A program may use at most 64 MiB of HBM per device.

v0:
```python
import jax
import jax.numpy as jnp
from jax import lax
from jax.sharding import PartitionSpec as P

OBS = 8192


def append_block(gathered, section):
    return jnp.dot(
        section, gathered, precision=lax.Precision.HIGHEST, preferred_element_type=jnp.float32
    )


def remove_block(gathered, running, section):
    return running - jnp.dot(
        section, gathered, precision=lax.Precision.HIGHEST, preferred_element_type=jnp.float32
    )


def body(lower, dinv, kcols, prior):
    segments = kcols.shape[0]
    breadth = kcols.shape[2]
    bounds = [(0, breadth)]
    pending = [
        [kcols[segment_now, :, bound_pair[0] : bound_pair[1]] for segment_now in range(segments)]
        for bound_pair in bounds
    ]
    spread = [[] for bound_pair in bounds]
    solved = [[] for bound_pair in bounds]
    for segment_now in range(segments):
        residual = pending[0][segment_now]
        for earlier in range(segment_now):
            residual = remove_block(
                spread[0][earlier],
                residual,
                lax.all_gather(
                    lower[segment_now * (segment_now - 1) // 2 + earlier], "col", axis=1, tiled=True
                ),
            )
        whole_residual = lax.all_gather(residual, "row", axis=0, tiled=True)
        answer = append_block(
            whole_residual, lax.all_gather(dinv[segment_now], "col", axis=1, tiled=True)
        )
        solved[0].append(answer)
        if segment_now + 1 < segments:
            whole_answer = lax.all_gather(answer, "row", axis=0, tiled=True)
            spread[0].append(whole_answer)
    columns = [solved[0][segment_now] for segment_now in range(segments)]
    solution = jnp.stack(columns)
    squares = jnp.sum(solution * solution, axis=(0, 1))
    totals = lax.psum(squares, "row")
    variance = prior - totals / OBS
    return (solution, variance)


def solution(mesh):
    in_specs = (P(None, "row", "col"), P(None, "row", "col"), P(None, "row", "col"), P("col"))
    out_specs = (P(None, "row", "col"), P("col"))
    return jax.shard_map(body, mesh=mesh, in_specs=in_specs, out_specs=out_specs, check_vma=False)
```

profile of v0, /device:TPU:2, one launch (start us, length us, event | category | flops | bytes accessed | tf_op | source)
XLA Modules:
  0.0 652.7 jit_solution(342715879217123548)
XLA Ops:
  7.2 0.0 copy-start.4
  7.2 0.0 all-gather.31.cloned.1.call-start
  7.2 1.5 slice.43
  8.7 0.0 all-gather.31.cloned.1.call-update
  8.8 0.0 all-gather.19.cloned.1.call-start
  8.8 1.0 fusion.21
  9.8 13.2 %all-gather = f32[1,64,2048]{2,1,0:T(8,128)S(1)} all-gather(f32[1,64,256]{2,1,0:T(8,128)S(1)} %get-tuple-element.12), channel_id=2, replica_groups=mesh['row'=32,'col'=8] {'col'}, dimensions={2}, use_global_device_ids=true | all-gather | bytes 589824 | tf_op jit(solution)/shard_map/all_gather | solution.py:43
  22.9 69.1 %all-gather.31.cloned.1.call-done = f32[1,2048,256]{2,1,0:T(8,128)} async-done(((f32[1,64,256]{2,1,0:T(8,128)}), f32[1,2048,256]{2,1,0:T(8,128)}) %all-gather.31.cloned.1.call-update) | async-done | bytes 2097168 | tf_op jit(solution)/shard_map/all_gather | solution.py:41
  92.1 3.4 fusion
  95.5 0.0 all-gather.19.cloned.1.call-update
  95.5 0.0 all-gather.21.cloned.1.call-start
  95.5 0.0 copy-done.4
  95.6 13.1 %all-gather.2 = f32[1,64,2048]{2,1,0:T(8,128)S(1)} all-gather(f32[1,64,256]{2,1,0:T(8,128)S(1)} %get-tuple-element.7), channel_id=4, replica_groups=mesh['row'=32,'col'=8] {'col'}, dimensions={2}, use_global_device_ids=true | all-gather | bytes 589824 | tf_op jit(solution)/shard_map/all_gather | solution.py:37
  108.7 62.1 %all-gather.19.cloned.1.call-done = f32[2048,256]{1,0:T(8,128)} async-done(((f32[64,256]{1,0:T(8,128)}), f32[2048,256]{1,0:T(8,128)}) %all-gather.19.cloned.1.call-update) | async-done | bytes 2097168 | tf_op jit(solution)/shard_map/all_gather | solution.py:47
  170.8 3.6 fusion.2
  174.3 0.0 all-gather.21.cloned.1.call-update
  174.4 0.0 all-gather.23.cloned.1.call-start
  174.4 13.1 %all-gather.3 = f32[1,64,2048]{2,1,0:T(8,128)S(1)} all-gather(f32[1,64,256]{2,1,0:T(8,128)S(1)} %get-tuple-element.11), channel_id=5, replica_groups=mesh['row'=32,'col'=8] {'col'}, dimensions={2}, use_global_device_ids=true | all-gather | bytes 589824 | tf_op jit(solution)/shard_map/all_gather | solution.py:43
  187.5 62.1 %all-gather.21.cloned.1.call-done = f32[2048,256]{1,0:T(8,128)} async-done(((f32[64,256]{1,0:T(8,128)}), f32[2048,256]{1,0:T(8,128)}) %all-gather.21.cloned.1.call-update) | async-done | bytes 2097168 | tf_op jit(solution)/shard_map/all_gather | solution.py:41
  249.7 3.6 fusion.16
  253.2 0.0 copy-start
  253.2 0.0 all-gather.23.cloned.1.call-update
  253.2 0.0 all-gather.25.cloned.1.call-start
  253.3 13.3 %all-gather.5 = f32[1,64,2048]{2,1,0:T(8,128)S(1)} all-gather(f32[1,64,256]{2,1,0:T(8,128)S(1)} %get-tuple-element.5), channel_id=7, replica_groups=mesh['row'=32,'col'=8] {'col'}, dimensions={2}, use_global_device_ids=true | all-gather | bytes 589824 | tf_op jit(solution)/shard_map/all_gather | solution.py:37
  266.5 13.1 %all-gather.4 = f32[1,64,2048]{2,1,0:T(8,128)S(1)} all-gather(f32[1,64,256]{2,1,0:T(8,128)S(1)} %get-tuple-element.6), channel_id=6, replica_groups=mesh['row'=32,'col'=8] {'col'}, dimensions={2}, use_global_device_ids=true | all-gather | bytes 589824 | tf_op jit(solution)/shard_map/all_gather | solution.py:37
  279.6 48.9 %all-gather.23.cloned.1.call-done = f32[2048,256]{1,0:T(8,128)} async-done(((f32[64,256]{1,0:T(8,128)}), f32[2048,256]{1,0:T(8,128)}) %all-gather.23.cloned.1.call-update) | async-done | bytes 2097168 | tf_op jit(solution)/shard_map/all_gather | solution.py:47
  328.5 2.9 convolution_bitcast_fusion.4
  331.4 0.0 copy-done
  331.4 2.8 fusion.4
  334.3 0.0 all-gather.25.cloned.1.call-update
  334.3 0.0 all-gather.27.cloned.1.call-start
  334.3 13.1 %all-gather.6 = f32[1,64,2048]{2,1,0:T(8,128)S(1)} all-gather(f32[1,64,256]{2,1,0:T(8,128)S(1)} %get-tuple-element.13), channel_id=8, replica_groups=mesh['row'=32,'col'=8] {'col'}, dimensions={2}, use_global_device_ids=true | all-gather | bytes 589824 | tf_op jit(solution)/shard_map/all_gather | solution.py:43
  347.4 62.1 %all-gather.25.cloned.1.call-done = f32[2048,256]{1,0:T(8,128)} async-done(((f32[64,256]{1,0:T(8,128)}), f32[2048,256]{1,0:T(8,128)}) %all-gather.25.cloned.1.call-update) | async-done | bytes 2097168 | tf_op jit(solution)/shard_map/all_gather | solution.py:41
  409.6 3.6 fusion.12
  413.1 0.0 all-gather.27.cloned.1.call-update
  413.2 0.0 all-gather.29.cloned.1.call-start
  413.2 13.1 %all-gather.9 = f32[1,64,2048]{2,1,0:T(8,128)S(1)} all-gather(f32[1,64,256]{2,1,0:T(8,128)S(1)} %get-tuple-element.8), channel_id=11, replica_groups=mesh['row'=32,'col'=8] {'col'}, dimensions={2}, use_global_device_ids=true | all-gather | bytes 589824 | tf_op jit(solution)/shard_map/all_gather | solution.py:37
  426.3 13.3 %all-gather.8 = f32[1,64,2048]{2,1,0:T(8,128)S(1)} all-gather(f32[1,64,256]{2,1,0:T(8,128)S(1)} %get-tuple-element.9), channel_id=10, replica_groups=mesh['row'=32,'col'=8] {'col'}, dimensions={2}, use_global_device_ids=true | all-gather | bytes 589824 | tf_op jit(solution)/shard_map/all_gather | solution.py:37
  439.6 13.1 %all-gather.7 = f32[1,64,2048]{2,1,0:T(8,128)S(1)} all-gather(f32[1,64,256]{2,1,0:T(8,128)S(1)} %get-tuple-element.4), channel_id=9, replica_groups=mesh['row'=32,'col'=8] {'col'}, dimensions={2}, use_global_device_ids=true | all-gather | bytes 589824 | tf_op jit(solution)/shard_map/all_gather | solution.py:37
  452.7 2.9 convolution_bitcast_fusion.2
  455.6 32.8 %all-gather.27.cloned.1.call-done = f32[2048,256]{1,0:T(8,128)} async-done(((f32[64,256]{1,0:T(8,128)}), f32[2048,256]{1,0:T(8,128)}) %all-gather.27.cloned.1.call-update) | async-done | bytes 2097168 | tf_op jit(solution)/shard_map/all_gather | solution.py:47
  488.4 2.9 convolution_bitcast_fusion.1
  491.3 2.8 fusion.7
  494.2 0.0 copy-start.1
  494.2 0.0 copy-start.2
  494.2 0.0 copy-start.3
  494.2 0.0 copy-start.5
  494.2 0.0 all-gather.29.cloned.1.call-update
  494.2 13.3 %all-gather.10 = f32[1,64,2048]{2,1,0:T(8,128)S(1)} all-gather(f32[1,64,256]{2,1,0:T(8,128)S(1)} %get-tuple-element.10), channel_id=12, replica_groups=mesh['row'=32,'col'=8] {'col'}, dimensions={2}, use_global_device_ids=true | all-gather | bytes 589824 | tf_op jit(solution)/shard_map/all_gather | solution.py:43
  507.4 62.0 %all-gather.29.cloned.1.call-done = f32[2048,256]{1,0:T(8,128)} async-done(((f32[64,256]{1,0:T(8,128)}), f32[2048,256]{1,0:T(8,128)}) %all-gather.29.cloned.1.call-update) | async-done | bytes 2097168 | tf_op jit(solution)/shard_map/all_gather | solution.py:41
  569.5 2.9 convolution_bitcast_fusion
  572.4 0.0 copy-done.1
  572.4 0.0 copy-done.2
  572.4 0.0 copy-done.3
  572.4 0.7 multiply_reduce_fusion
  573.2 72.1 %psum.7 = f32[256]{0:T(256)S(1)} all-reduce(f32[256]{0:T(256)S(1)} %get-tuple-element.2), channel_id=1, replica_groups=mesh['row'=32,'col'=8] {'row'}, use_global_device_ids=true, to_apply=%region_1.0 | all-reduce | flops 256 | bytes 2048 | tf_op jit(solution)/shard_map/psum | solution.py:52
  645.3 0.0 copy-done.5
  645.3 0.6 multiply_subtract_fusion
  (1 shorter events, 0.0 us)
Async XLA Ops:
  7.2 88.4 %copy-start.4 = (f32[6,64,256]{2,1,0:T(8,128)S(1)}, f32[6,64,256]{2,1,0:T(8,128)}, u32[]{:S(2)}) copy-start(f32[6,64,256]{2,1,0:T(8,128)} %param.4) | copy-start | bytes 1179652
  7.2 84.9 %all-gather.31.cloned.1.call-start = ((), (), s32[]{:S(2)}) async-start(), calls=%async_computation.6 | async-start | bytes 2162688 | tf_op jit(solution)/shard_map/all_gather | solution.py:41
  8.8 162.0 %all-gather.19.cloned.1.call-start = ((), (), s32[]{:S(2)}) async-start(), calls=%async_computation | async-start | bytes 2162688 | tf_op jit(solution)/shard_map/all_gather | solution.py:47
  95.5 154.2 %all-gather.21.cloned.1.call-start = ((), (), s32[]{:S(2)}) async-start(), calls=%async_computation.1 | async-start | bytes 2162688 | tf_op jit(solution)/shard_map/all_gather | solution.py:41
  174.4 154.1 %all-gather.23.cloned.1.call-start = ((), (), s32[]{:S(2)}) async-start(), calls=%async_computation.2 | async-start | bytes 2162688 | tf_op jit(solution)/shard_map/all_gather | solution.py:47
  253.2 78.2 %copy-start = (f32[2048,256]{1,0:T(8,128)S(1)}, f32[2048,256]{1,0:T(8,128)}, u32[]{:S(2)}) copy-start(f32[2048,256]{1,0:T(8,128)} %all-gather.19.cloned.1.call-done) | copy-start | bytes 6291460
  253.2 156.3 %all-gather.25.cloned.1.call-start = ((), (), s32[]{:S(2)}) async-start(), calls=%async_computation.3 | async-start | bytes 2162688 | tf_op jit(solution)/shard_map/all_gather | solution.py:41
  334.3 154.1 %all-gather.27.cloned.1.call-start = ((), (), s32[]{:S(2)}) async-start(), calls=%async_computation.4 | async-start | bytes 2162688 | tf_op jit(solution)/shard_map/all_gather | solution.py:47
  413.2 156.3 %all-gather.29.cloned.1.call-start = ((), (), s32[]{:S(2)}) async-start(), calls=%async_computation.5 | async-start | bytes 2162688 | tf_op jit(solution)/shard_map/all_gather | solution.py:41
  494.2 78.3 %copy-start.1 = (f32[64,256]{1,0:T(8,128)S(1)}, f32[64,256]{1,0:T(8,128)}, u32[]{:S(2)}) copy-start(f32[64,256]{1,0:T(8,128)} %fusion) | copy-start | bytes 196612
  494.2 78.3 %copy-start.2 = (f32[256,64]{0,1:T(8,128)S(1)}, f32[256,64]{0,1:T(8,128)}, u32[]{:S(2)}) copy-start(f32[256,64]{0,1:T(8,128)} %fusion.16) | copy-start | bytes 196612
  494.2 78.3 %copy-start.3 = (f32[256,64]{0,1:T(8,128)S(1)}, f32[256,64]{0,1:T(8,128)}, u32[]{:S(2)}) copy-start(f32[256,64]{0,1:T(8,128)} %fusion.12) | copy-start | bytes 196612
  494.2 151.1 %copy-start.5 = (f32[256]{0:T(256)S(1)}, f32[256]{0:T(256)}, u32[]{:S(2)}) copy-start(f32[256]{0:T(256)} %param.7) | copy-start | bytes 3076
Sparse Core Ops, SparseCore 0:
  11.2 80.8 all-gather.30
  95.6 75.1 all-gather.18
  174.5 75.1 all-gather.20
  253.4 75.0 all-gather.22
  334.4 75.1 all-gather.24
  413.3 75.0 all-gather.26
  494.3 75.1 all-gather.28
where the time goes:
time: 653 us
  waiting for transfers between devices  399 us (61%)
  blocking collectives  204 us (31%)
  matrix products  31.4 us (5%)
  between operations  14.2 us (2%)
    all_gather x4, waiting for transfers between devices, body(): whole_residual = lax.all_gather(residual, 'row', axis=0, tiled=True)  255 us
    all_gather x3, waiting for transfers between devices, body(): whole_answer = lax.all_gather(answer, 'row', axis=0, tiled=True)  144 us
    all_gather x6, blocking collectives, body(): lax.all_gather(lower[segment_now * (segment_now - 1) // 2 + earlier], 'co...  78.9 us
    psum x1, blocking collectives, body(): totals = lax.psum(squares, 'row')  72.1 us
    all_gather x4, blocking collectives, body(): lax.all_gather(dinv[segment_now], 'col', axis=1, tiled=True)  52.7 us
    dot_general x6, matrix products, remove_block(): jnp.dot(section, gathered, precision=lax.Precision.HIGHEST, preferred_ele...  18 us
    dot_general x4, matrix products, append_block(): jnp.dot(section, gathered, precision=lax.Precision.HIGHEST, preferred_ele...  13.4 us
  transfers between devices with their start and end apart: 7, of which 7 were waited for; matrix products, arithmetic and copies ran while one was open for 1% of the time, Pallas kernels for 0%

commit v1 on v0

--- a/solution.py
+++ b/solution.py
@@ -49,7 +49,7 @@
     columns = [solved[0][segment_now] for segment_now in range(segments)]
     solution = jnp.stack(columns)
     squares = jnp.sum(solution * solution, axis=(0, 1))
-    totals = lax.psum(squares, "row")
+    totals = jnp.sum(lax.all_gather(squares, "row"), axis=0)
     variance = prior - totals / OBS
     return (solution, variance)
 

time: 653 us -> 623 us (0.954)
  blocking collectives: 204 us -> 173 us
    psum x1 -> x0, blocking collectives: 72.1 us -> none  [body(): totals = lax.psum(squares, 'row')]
    all_gather x0 -> x1, blocking collectives: none -> 41.4 us  [body(): totals = jnp.sum(lax.all_gather(squares, 'row'), axis=0)]
where the time goes in v1:
time: 623 us; the launch traced here: 622 us
  waiting for transfers between devices  399 us (64%)
  blocking collectives  173 us (28%)
  matrix products  31.4 us (5%)
  between operations  14.2 us (2%)
    all_gather x4, waiting for transfers between devices, body(): whole_residual = lax.all_gather(residual, 'row', axis=0, tiled=True)  255 us
    all_gather x3, waiting for transfers between devices, body(): whole_answer = lax.all_gather(answer, 'row', axis=0, tiled=True)  144 us
    all_gather x6, blocking collectives, body(): lax.all_gather(lower[segment_now * (segment_now - 1) // 2 + earlier], 'co...  78.9 us
    all_gather x4, blocking collectives, body(): lax.all_gather(dinv[segment_now], 'col', axis=1, tiled=True)  52.7 us
    all_gather x1, blocking collectives, body(): totals = jnp.sum(lax.all_gather(squares, 'row'), axis=0)  41.4 us
    dot_general x6, matrix products, remove_block(): jnp.dot(section, gathered, precision=lax.Precision.HIGHEST, preferred_ele...  18 us
    dot_general x4, matrix products, append_block(): jnp.dot(section, gathered, precision=lax.Precision.HIGHEST, preferred_ele...  13.4 us
  transfers between devices with their start and end apart: 7, of which 7 were waited for; matrix products, arithmetic and copies ran while one was open for 1% of the time, Pallas kernels for 0%

profile of v1, /device:TPU:2, one launch (start us, length us, event | category | flops | bytes accessed | tf_op | source)
XLA Modules:
  0.0 622.0 jit_solution(9787383809575806575)
XLA Ops:
  7.2 0.0 copy-start.4
  7.2 0.0 all-gather.33.cloned.1.call-start
  7.2 1.5 slice.43
  8.7 0.0 all-gather.33.cloned.1.call-update
  8.8 0.0 all-gather.21.cloned.1.call-start
  8.8 1.0 fusion.21
  9.8 13.2 %all-gather = f32[1,64,2048]{2,1,0:T(8,128)S(1)} all-gather(f32[1,64,256]{2,1,0:T(8,128)S(1)} %get-tuple-element.12), channel_id=2, replica_groups=mesh['row'=32,'col'=8] {'col'}, dimensions={2}, use_global_device_ids=true | all-gather | bytes 589824 | tf_op jit(solution)/shard_map/all_gather | solution.py:43
  22.9 69.1 %all-gather.33.cloned.1.call-done = f32[1,2048,256]{2,1,0:T(8,128)} async-done(((f32[1,64,256]{2,1,0:T(8,128)}), f32[1,2048,256]{2,1,0:T(8,128)}) %all-gather.33.cloned.1.call-update) | async-done | bytes 2097168 | tf_op jit(solution)/shard_map/all_gather | solution.py:41
  92.1 3.4 fusion
  95.5 0.0 all-gather.21.cloned.1.call-update
  95.5 0.0 all-gather.23.cloned.1.call-start
  95.5 0.0 copy-done.4
  95.6 13.1 %all-gather.2 = f32[1,64,2048]{2,1,0:T(8,128)S(1)} all-gather(f32[1,64,256]{2,1,0:T(8,128)S(1)} %get-tuple-element.7), channel_id=4, replica_groups=mesh['row'=32,'col'=8] {'col'}, dimensions={2}, use_global_device_ids=true | all-gather | bytes 589824 | tf_op jit(solution)/shard_map/all_gather | solution.py:37
  108.7 62.1 %all-gather.21.cloned.1.call-done = f32[2048,256]{1,0:T(8,128)} async-done(((f32[64,256]{1,0:T(8,128)}), f32[2048,256]{1,0:T(8,128)}) %all-gather.21.cloned.1.call-update) | async-done | bytes 2097168 | tf_op jit(solution)/shard_map/all_gather | solution.py:47
  170.8 3.6 fusion.2
  174.3 0.0 all-gather.23.cloned.1.call-update
  174.4 0.0 all-gather.25.cloned.1.call-start
  174.4 13.1 %all-gather.3 = f32[1,64,2048]{2,1,0:T(8,128)S(1)} all-gather(f32[1,64,256]{2,1,0:T(8,128)S(1)} %get-tuple-element.11), channel_id=5, replica_groups=mesh['row'=32,'col'=8] {'col'}, dimensions={2}, use_global_device_ids=true | all-gather | bytes 589824 | tf_op jit(solution)/shard_map/all_gather | solution.py:43
  187.5 62.1 %all-gather.23.cloned.1.call-done = f32[2048,256]{1,0:T(8,128)} async-done(((f32[64,256]{1,0:T(8,128)}), f32[2048,256]{1,0:T(8,128)}) %all-gather.23.cloned.1.call-update) | async-done | bytes 2097168 | tf_op jit(solution)/shard_map/all_gather | solution.py:41
  249.7 3.6 fusion.16
  253.2 0.0 copy-start
  253.2 0.0 all-gather.25.cloned.1.call-update
  253.2 0.0 all-gather.27.cloned.1.call-start
  253.3 13.3 %all-gather.5 = f32[1,64,2048]{2,1,0:T(8,128)S(1)} all-gather(f32[1,64,256]{2,1,0:T(8,128)S(1)} %get-tuple-element.5), channel_id=7, replica_groups=mesh['row'=32,'col'=8] {'col'}, dimensions={2}, use_global_device_ids=true | all-gather | bytes 589824 | tf_op jit(solution)/shard_map/all_gather | solution.py:37
  266.5 13.1 %all-gather.4 = f32[1,64,2048]{2,1,0:T(8,128)S(1)} all-gather(f32[1,64,256]{2,1,0:T(8,128)S(1)} %get-tuple-element.6), channel_id=6, replica_groups=mesh['row'=32,'col'=8] {'col'}, dimensions={2}, use_global_device_ids=true | all-gather | bytes 589824 | tf_op jit(solution)/shard_map/all_gather | solution.py:37
  279.6 48.9 %all-gather.25.cloned.1.call-done = f32[2048,256]{1,0:T(8,128)} async-done(((f32[64,256]{1,0:T(8,128)}), f32[2048,256]{1,0:T(8,128)}) %all-gather.25.cloned.1.call-update) | async-done | bytes 2097168 | tf_op jit(solution)/shard_map/all_gather | solution.py:47
  328.5 2.9 convolution_bitcast_fusion.4
  331.4 0.0 copy-done
  331.4 2.8 fusion.4
  334.3 0.0 all-gather.27.cloned.1.call-update
  334.3 0.0 all-gather.29.cloned.1.call-start
  334.3 13.1 %all-gather.6 = f32[1,64,2048]{2,1,0:T(8,128)S(1)} all-gather(f32[1,64,256]{2,1,0:T(8,128)S(1)} %get-tuple-element.13), channel_id=8, replica_groups=mesh['row'=32,'col'=8] {'col'}, dimensions={2}, use_global_device_ids=true | all-gather | bytes 589824 | tf_op jit(solution)/shard_map/all_gather | solution.py:43
  347.4 62.1 %all-gather.27.cloned.1.call-done = f32[2048,256]{1,0:T(8,128)} async-done(((f32[64,256]{1,0:T(8,128)}), f32[2048,256]{1,0:T(8,128)}) %all-gather.27.cloned.1.call-update) | async-done | bytes 2097168 | tf_op jit(solution)/shard_map/all_gather | solution.py:41
  409.6 3.6 fusion.12
  413.1 0.0 all-gather.29.cloned.1.call-update
  413.2 0.0 all-gather.31.cloned.1.call-start
  413.2 13.1 %all-gather.9 = f32[1,64,2048]{2,1,0:T(8,128)S(1)} all-gather(f32[1,64,256]{2,1,0:T(8,128)S(1)} %get-tuple-element.8), channel_id=11, replica_groups=mesh['row'=32,'col'=8] {'col'}, dimensions={2}, use_global_device_ids=true | all-gather | bytes 589824 | tf_op jit(solution)/shard_map/all_gather | solution.py:37
  426.3 13.3 %all-gather.8 = f32[1,64,2048]{2,1,0:T(8,128)S(1)} all-gather(f32[1,64,256]{2,1,0:T(8,128)S(1)} %get-tuple-element.9), channel_id=10, replica_groups=mesh['row'=32,'col'=8] {'col'}, dimensions={2}, use_global_device_ids=true | all-gather | bytes 589824 | tf_op jit(solution)/shard_map/all_gather | solution.py:37
  439.6 13.1 %all-gather.7 = f32[1,64,2048]{2,1,0:T(8,128)S(1)} all-gather(f32[1,64,256]{2,1,0:T(8,128)S(1)} %get-tuple-element.4), channel_id=9, replica_groups=mesh['row'=32,'col'=8] {'col'}, dimensions={2}, use_global_device_ids=true | all-gather | bytes 589824 | tf_op jit(solution)/shard_map/all_gather | solution.py:37
  452.7 2.9 convolution_bitcast_fusion.2
  455.6 32.8 %all-gather.29.cloned.1.call-done = f32[2048,256]{1,0:T(8,128)} async-done(((f32[64,256]{1,0:T(8,128)}), f32[2048,256]{1,0:T(8,128)}) %all-gather.29.cloned.1.call-update) | async-done | bytes 2097168 | tf_op jit(solution)/shard_map/all_gather | solution.py:47
  488.4 2.9 convolution_bitcast_fusion.1
  491.3 2.8 fusion.7
  494.2 0.0 copy-start.1
  494.2 0.0 copy-start.2
  494.2 0.0 copy-start.3
  494.2 0.0 copy-start.5
  494.2 0.0 all-gather.31.cloned.1.call-update
  494.2 13.3 %all-gather.10 = f32[1,64,2048]{2,1,0:T(8,128)S(1)} all-gather(f32[1,64,256]{2,1,0:T(8,128)S(1)} %get-tuple-element.10), channel_id=12, replica_groups=mesh['row'=32,'col'=8] {'col'}, dimensions={2}, use_global_device_ids=true | all-gather | bytes 589824 | tf_op jit(solution)/shard_map/all_gather | solution.py:43
  507.4 62.0 %all-gather.31.cloned.1.call-done = f32[2048,256]{1,0:T(8,128)} async-done(((f32[64,256]{1,0:T(8,128)}), f32[2048,256]{1,0:T(8,128)}) %all-gather.31.cloned.1.call-update) | async-done | bytes 2097168 | tf_op jit(solution)/shard_map/all_gather | solution.py:41
  569.5 2.9 convolution_bitcast_fusion
  572.4 0.0 copy-done.1
  572.4 0.0 copy-done.2
  572.4 0.0 copy-done.3
  572.4 0.7 multiply_reduce_fusion
  573.2 41.4 %all-gather.12 = f32[32,1,256]{2,1,0:T(1,128)S(1)} all-gather(f32[1,1,256]{2,1,0:T(1,128)S(1)} %bitcast.89), channel_id=13, replica_groups=mesh['row'=32,'col'=8] {'row'}, dimensions={0}, use_global_device_ids=true | all-gather | bytes 33792 | tf_op jit(solution)/shard_map/all_gather | solution.py:52
  614.5 0.1 reduce_sum.19
  614.6 0.0 copy-done.5
  614.6 0.6 multiply_subtract_fusion
  (1 shorter events, 0.0 us)
Async XLA Ops:
  7.2 88.4 %copy-start.4 = (f32[6,64,256]{2,1,0:T(8,128)S(1)}, f32[6,64,256]{2,1,0:T(8,128)}, u32[]{:S(2)}) copy-start(f32[6,64,256]{2,1,0:T(8,128)} %param.4) | copy-start | bytes 1179652
  7.2 84.9 %all-gather.33.cloned.1.call-start = ((), (), s32[]{:S(2)}) async-start(), calls=%async_computation.6 | async-start | bytes 2162688 | tf_op jit(solution)/shard_map/all_gather | solution.py:41
  8.8 162.0 %all-gather.21.cloned.1.call-start = ((), (), s32[]{:S(2)}) async-start(), calls=%async_computation | async-start | bytes 2162688 | tf_op jit(solution)/shard_map/all_gather | solution.py:47
  95.5 154.2 %all-gather.23.cloned.1.call-start = ((), (), s32[]{:S(2)}) async-start(), calls=%async_computation.1 | async-start | bytes 2162688 | tf_op jit(solution)/shard_map/all_gather | solution.py:41
  174.4 154.1 %all-gather.25.cloned.1.call-start = ((), (), s32[]{:S(2)}) async-start(), calls=%async_computation.2 | async-start | bytes 2162688 | tf_op jit(solution)/shard_map/all_gather | solution.py:47
  253.2 78.2 %copy-start = (f32[2048,256]{1,0:T(8,128)S(1)}, f32[2048,256]{1,0:T(8,128)}, u32[]{:S(2)}) copy-start(f32[2048,256]{1,0:T(8,128)} %all-gather.21.cloned.1.call-done) | copy-start | bytes 6291460
  253.2 156.3 %all-gather.27.cloned.1.call-start = ((), (), s32[]{:S(2)}) async-start(), calls=%async_computation.3 | async-start | bytes 2162688 | tf_op jit(solution)/shard_map/all_gather | solution.py:41
  334.3 154.1 %all-gather.29.cloned.1.call-start = ((), (), s32[]{:S(2)}) async-start(), calls=%async_computation.4 | async-start | bytes 2162688 | tf_op jit(solution)/shard_map/all_gather | solution.py:47
  413.2 156.3 %all-gather.31.cloned.1.call-start = ((), (), s32[]{:S(2)}) async-start(), calls=%async_computation.5 | async-start | bytes 2162688 | tf_op jit(solution)/shard_map/all_gather | solution.py:41
  494.2 78.3 %copy-start.1 = (f32[64,256]{1,0:T(8,128)S(1)}, f32[64,256]{1,0:T(8,128)}, u32[]{:S(2)}) copy-start(f32[64,256]{1,0:T(8,128)} %fusion) | copy-start | bytes 196612
  494.2 78.3 %copy-start.2 = (f32[256,64]{0,1:T(8,128)S(1)}, f32[256,64]{0,1:T(8,128)}, u32[]{:S(2)}) copy-start(f32[256,64]{0,1:T(8,128)} %fusion.16) | copy-start | bytes 196612
  494.2 78.3 %copy-start.3 = (f32[256,64]{0,1:T(8,128)S(1)}, f32[256,64]{0,1:T(8,128)}, u32[]{:S(2)}) copy-start(f32[256,64]{0,1:T(8,128)} %fusion.12) | copy-start | bytes 196612
  494.2 120.4 %copy-start.5 = (f32[256]{0:T(256)S(1)}, f32[256]{0:T(256)}, u32[]{:S(2)}) copy-start(f32[256]{0:T(256)} %param.7) | copy-start | bytes 3076
Sparse Core Ops, SparseCore 0:
  11.2 80.8 all-gather.32
  95.6 75.1 all-gather.20
  174.5 75.1 all-gather.22
  253.4 75.0 all-gather.24
  334.4 75.1 all-gather.26
  413.3 75.0 all-gather.28
  494.3 75.1 all-gather.30
